TPU v7x, 128 devices: a whole 4x4x4 slice. The times are simulated.
128 devices in a mesh: mem: 16 (over z, y), cell: 8 (over x, core).
Axes of the slice: x: 4, y: 4, z: 4, core: 2. Of those that a mesh axis runs over, the one named last changes fastest.
Arguments:
- turnover_effect: float32 [1024, 65536], P('mem', 'cell'), may hold values from -3 to 3
- base_rate: float32 [65536], P('cell'), may hold values from 0.05 to 0.5
- fast_rate: float32 [65536], P('cell'), may hold values from 0.02 to 0.2
- slow_rate: float32 [65536], P('cell'), may hold values from 0.005 to 0.05
- init_pools: float32 [3, 65536], P(None, 'cell'), may hold values from 1 to 6
- litterfall: float32 [6, 65536], P(None, 'cell'), may hold values from 0.1 to 1
- obs_taps: int32 [16384, 4], P('cell'), may hold values from 0 to 127
- obs_weights: float32 [16384, 4], P('cell'), may hold values from 0.05 to 0.5
- observed: float32 [16384], P('cell'), may hold values from 0.5 to 4
- obs_var: float32 [16384], P('cell'), may hold values from 0.008 to 0.11, as said below
- obs_noise: float32 [1024, 16384], P('mem', 'cell'), may hold values from -6 to 6
Outputs:
- updated_effect: float32 [1024, 65536], P('mem', 'cell')
Inputs may be any that keep to these rules, and one draw needn't show every extreme that they name: `obs_var`: positive variances.
All inputs are finite; a program needn't handle non-finite values.
Results may differ from a plain program's by a relative error of at most 0.00025.
Values sent between devices are 32-bit elements; how exact they have to be, the bound alone decides.
No kernel may reach another device: no remote copies, remote signals or barrier semaphores. Data moves between devices by JAX's collectives and lax.ppermute only.
A program may use at most 192 MiB of HBM per device.

v0:
```python
import math
import jax
import jax.numpy as jnp
from jax import lax
from jax.sharding import PartitionSpec as P

STEPS = 6
BLOCK = 128
TAPS = 4
highest = lax.Precision.HIGHEST


def forward(turnover_effect, base_rate, fast_rate, slow_rate, init_pools, litterfall):
    decayed = 1.0 - jnp.exp(-base_rate[None, :] * jnp.exp(turnover_effect))
    litter = jnp.broadcast_to(init_pools[0][None, :], turnover_effect.shape)
    fast_pool = jnp.broadcast_to(init_pools[1][None, :], turnover_effect.shape)
    slow_pool = jnp.broadcast_to(init_pools[2][None, :], turnover_effect.shape)
    resp_total = jnp.zeros(turnover_effect.shape, jnp.float32)
    for month in range(STEPS):
        litter_out = decayed * litter
        fast_out = fast_rate[None, :] * fast_pool
        slow_out = slow_rate[None, :] * slow_pool
        resp_total = resp_total + 0.6 * litter_out + 0.7 * fast_out + slow_out
        litter = litter - litter_out + litterfall[month][None, :]
        fast_pool = fast_pool + 0.4 * litter_out - fast_out
        slow_pool = slow_pool + 0.3 * fast_out - slow_out
    return resp_total


def observe(resp_total, obs_taps, obs_weights):
    member_count = resp_total.shape[0]
    block_count = resp_total.shape[1] // BLOCK
    positions = jnp.arange(BLOCK, dtype=jnp.int32)
    operator_table = jnp.zeros((obs_taps.shape[0], BLOCK), jnp.float32)
    for tap_index in range(TAPS):
        hits = (obs_taps[:, tap_index][:, None] == positions[None, :]).astype(jnp.float32)
        operator_table = operator_table + obs_weights[:, tap_index][:, None] * hits
    operator_table = operator_table.reshape(block_count, -1, BLOCK)
    blocked = resp_total.reshape(member_count, block_count, BLOCK)
    predicted = jnp.einsum("jbc,boc->jbo", blocked, operator_table, precision=highest)
    return predicted.reshape(member_count, -1)


def spd_solve(matrix, right_side):
    factor = jnp.linalg.cholesky(matrix)
    halfway = lax.linalg.triangular_solve(factor, right_side, left_side=True, lower=True)
    return lax.linalg.triangular_solve(
        factor, halfway, left_side=True, lower=True, transpose_a=True
    )


def contract_last(left, right):
    return lax.dot_general(left, right, (((1,), (1,)), ((), ())), precision=highest)


def body(
    turnover_effect,
    base_rate,
    fast_rate,
    slow_rate,
    init_pools,
    litterfall,
    obs_taps,
    obs_weights,
    observed,
    obs_var,
    obs_noise,
):
    resp_total = forward(turnover_effect, base_rate, fast_rate, slow_rate, init_pools, litterfall)
    predicted = observe(resp_total, obs_taps, obs_weights)
    mem_count = lax.axis_size("mem")
    cell_count = lax.axis_size("cell")
    local_members, local_cells = turnover_effect.shape
    local_obs = predicted.shape[1]
    member_count = local_members * mem_count
    all_obs = local_obs * cell_count
    inv_root = 1.0 / math.sqrt(member_count - 1)
    effect_sum, predicted_sum = lax.psum(
        (jnp.sum(turnover_effect, axis=0), jnp.sum(predicted, axis=0)), "mem"
    )
    anomaly = (turnover_effect - (effect_sum / member_count)[None, :]) * inv_root
    pred_anomaly = (predicted - (predicted_sum / member_count)[None, :]) * inv_root
    residual = observed[None, :] - predicted
    misfit_local = jnp.sum(residual * residual / obs_var[None, :])
    departure = observed[None, :] + jnp.sqrt(obs_var)[None, :] * obs_noise - predicted
    identity_matrix = jnp.eye(member_count, dtype=jnp.float32)
    misfit_sum = lax.psum(misfit_local, ("mem", "cell"))
    stacked = jnp.concatenate(
        [pred_anomaly / obs_var[None, :], departure / obs_var[None, :]], axis=0
    )
    partial_cols = contract_last(lax.all_gather(pred_anomaly, "mem", axis=0, tiled=True), stacked)
    summed = lax.psum(partial_cols, "cell")
    gram = lax.all_gather(summed[:, :local_members], "mem", axis=1, tiled=True)
    step_size = member_count * all_obs / misfit_sum
    local_solve = spd_solve(
        identity_matrix + step_size * gram, step_size * summed[:, local_members:]
    )
    change = jnp.einsum(
        "kj,kc->jc",
        local_solve,
        lax.all_gather(anomaly, "mem", axis=0, tiled=True),
        precision=highest,
    )
    return turnover_effect + change


def solution(mesh):
    in_specs = (
        P("mem", "cell"),
        P("cell"),
        P("cell"),
        P("cell"),
        P(None, "cell"),
        P(None, "cell"),
        P("cell", None),
        P("cell", None),
        P("cell"),
        P("cell"),
        P("mem", "cell"),
    )
    out_specs = P("mem", "cell")
    return jax.shard_map(body, mesh=mesh, in_specs=in_specs, out_specs=out_specs, check_vma=False)
```

profile of v0, /device:TPU:1, one launch (start us, length us, event | category | flops | bytes accessed | tf_op | source)
XLA Modules:
  0.0 692.4 jit_solution(13496281260930924091)
XLA Ops:
  24.5 9.8 %fusion.32 = (f32[]{:T(128)}, f32[64,32]{1,0:T(8,128)S(1)}, f32[64,32,64]{2,1,0:T(8,128)S(1)}) fusion(f32[64,32]{1,0:T(8,128)S(1)} %div.48, f32[64,32]{1,0:T(8,128)S(1)} %sub.84, f32[8,64,8,128]{3,2,1,0:T(8,128)S(1)} %get-tuple-element.42, f32[64,32]{1,0:T(8,128)S(1)} %mul.268, s32[64,32]{1,0:T(8,128)S(1)} %eq.80, f32[64,32]{1,0:T(8,128)S(1)} %mul.265, ...), kind=kOutput, calls=%fused_computation.81 | convolution fusion | flops 204863488 | bytes 2711556 | tf_op jit(solution)/shard_map/jbc,boc->jbo/dot_general | solution.py:40
  34.3 62.6 %all-reduce.1 = (f32[2048]{0:T(1024)S(1)}, f32[8192]{0:T(1024)S(1)}) all-reduce(f32[2048]{0:T(1024)S(1)} %reduce_sum.31, f32[8192]{0:T(1024)S(1)} %get-tuple-element.41), channel_id=1, replica_groups=mesh['mem'=16,'cell'=8] {'mem'}, use_global_device_ids=true, to_apply=%region_3.0 | all-reduce | flops 10240 | bytes 81920 | tf_op jit(solution)/shard_map/psum | solution.py:78
  99.4 81.4 %all-gather.4.cloned.1.call-done = f32[1024,2048]{1,0:T(8,128)} async-done(((f32[64,2048]{1,0:T(8,128)}), f32[1024,2048]{1,0:T(8,128)}) %all-gather.4.cloned.1.call-update) | async-done | bytes 8388624 | tf_op jit(solution)/shard_map/all_gather | solution.py:91
  180.8 12.0 %fusion.19 = f32[1024,128]{0,1:T(8,128)} fusion(f32[1024,2048]{1,0:T(8,128)} %all-gather.4.cloned.1.call-done, f32[64,2048]{1,0:T(8,128)S(1)} %get-tuple-element.43, f32[64,2048]{1,0:T(8,128)S(1)} %get-tuple-element.33), kind=kOutput, calls=%fused_computation.62 | convolution fusion | flops 3221487616 | bytes 9961472 | tf_op jit(solution)/shard_map/dot_general | solution.py:53
  192.9 64.7 %psum.28 = f32[]{:T(128)} all-reduce(f32[]{:T(128)} %get-tuple-element.13), channel_id=1, replica_groups=mesh['mem'=16,'cell'=8] {'mem','cell'}, use_global_device_ids=true, to_apply=%region_1.0 | all-reduce | flops 1 | bytes 8 | tf_op jit(solution)/shard_map/psum | solution.py:87
  261.8 47.4 %all-gather.6.cloned.1.call-done = f32[1024,1024]{0,1:T(8,128)} async-done(((f32[1024,64]{0,1:T(8,128)}), f32[1024,1024]{0,1:T(8,128)}) %all-gather.6.cloned.1.call-update) | async-done | bytes 4194320 | tf_op jit(solution)/shard_map/all_gather | solution.py:93
  327.7 11.7 %cholesky.223 = f32[128,128]{1,0:T(8,128)S(1)} custom-call(f32[128,128]{1,0:T(8,128)S(1)} %cholesky.580), custom_call_target="Cholesky" | custom-call | tf_op jit(solution)/shard_map/jit(cholesky)/cholesky | solution.py:45
  341.9 9.8 %custom-call.64 = f32[1,128,128]{1,2,0:T(8,128)S(1)} custom-call(f32[1,128,128]{2,1,0:T(8,128)S(1)} %get-tuple-element.75), custom_call_target="InvertDiagBlocksLowerTriangular" | custom-call | tf_op jit(solution)/shard_map/jit(cholesky)/cholesky | solution.py:45
  355.6 11.8 %cholesky.244 = f32[128,128]{1,0:T(8,128)S(1)} custom-call(f32[128,128]{1,0:T(8,128)S(1)} %cholesky.584), custom_call_target="Cholesky" | custom-call | tf_op jit(solution)/shard_map/jit(cholesky)/cholesky | solution.py:45
  368.1 9.8 %custom-call.65 = f32[1,128,128]{1,2,0:T(8,128)S(1)} custom-call(f32[1,128,128]{2,1,0:T(8,128)S(1)} %get-tuple-element.72), custom_call_target="InvertDiagBlocksLowerTriangular" | custom-call | tf_op jit(solution)/shard_map/jit(cholesky)/cholesky | solution.py:45
  381.3 11.7 %cholesky.468 = f32[128,128]{1,0:T(8,128)S(1)} custom-call(f32[128,128]{1,0:T(8,128)S(1)} %cholesky.589), custom_call_target="Cholesky" | custom-call | tf_op jit(solution)/shard_map/jit(cholesky)/cholesky | solution.py:45
  393.6 9.8 %custom-call.66 = f32[1,128,128]{1,2,0:T(8,128)S(1)} custom-call(f32[1,128,128]{2,1,0:T(8,128)S(1)} %get-tuple-element.69), custom_call_target="InvertDiagBlocksLowerTriangular" | custom-call | tf_op jit(solution)/shard_map/jit(cholesky)/cholesky | solution.py:45
  407.0 11.9 %cholesky.487 = f32[128,128]{1,0:T(8,128)S(1)} custom-call(f32[128,128]{1,0:T(8,128)S(1)} %cholesky.594), custom_call_target="Cholesky" | custom-call | tf_op jit(solution)/shard_map/jit(cholesky)/cholesky | solution.py:45
  419.5 9.8 %custom-call.67 = f32[1,128,128]{1,2,0:T(8,128)S(1)} custom-call(f32[1,128,128]{2,1,0:T(8,128)S(1)} %get-tuple-element.66), custom_call_target="InvertDiagBlocksLowerTriangular" | custom-call | tf_op jit(solution)/shard_map/jit(cholesky)/cholesky | solution.py:45
  432.9 11.7 %cholesky.506 = f32[128,128]{1,0:T(8,128)S(1)} custom-call(f32[128,128]{1,0:T(8,128)S(1)} %cholesky.599), custom_call_target="Cholesky" | custom-call | tf_op jit(solution)/shard_map/jit(cholesky)/cholesky | solution.py:45
  445.2 10.2 %custom-call.68 = f32[1,128,128]{1,2,0:T(8,128)S(1)} custom-call(f32[1,128,128]{2,1,0:T(8,128)S(1)} %get-tuple-element.63), custom_call_target="InvertDiagBlocksLowerTriangular" | custom-call | tf_op jit(solution)/shard_map/jit(cholesky)/cholesky | solution.py:45
  458.8 11.7 %cholesky.526 = f32[128,128]{1,0:T(8,128)S(1)} custom-call(f32[128,128]{1,0:T(8,128)S(1)} %cholesky.604), custom_call_target="Cholesky" | custom-call | tf_op jit(solution)/shard_map/jit(cholesky)/cholesky | solution.py:45
  471.2 9.8 %custom-call.69 = f32[1,128,128]{1,2,0:T(8,128)S(1)} custom-call(f32[1,128,128]{2,1,0:T(8,128)S(1)} %get-tuple-element.60), custom_call_target="InvertDiagBlocksLowerTriangular" | custom-call | tf_op jit(solution)/shard_map/jit(cholesky)/cholesky | solution.py:45
  484.0 11.9 %cholesky.546 = f32[128,128]{1,0:T(8,128)S(1)} custom-call(f32[128,128]{1,0:T(8,128)S(1)} %cholesky.609), custom_call_target="Cholesky" | custom-call | tf_op jit(solution)/shard_map/jit(cholesky)/cholesky | solution.py:45
  496.5 9.8 %custom-call.70 = f32[1,128,128]{1,2,0:T(8,128)S(1)} custom-call(f32[1,128,128]{2,1,0:T(8,128)S(1)} %get-tuple-element.57), custom_call_target="InvertDiagBlocksLowerTriangular" | custom-call | tf_op jit(solution)/shard_map/jit(cholesky)/cholesky | solution.py:45
  509.0 11.7 %cholesky.564 = f32[128,128]{1,0:T(8,128)S(1)} custom-call(f32[128,128]{1,0:T(8,128)S(1)} %convolution_subtract_fusion.6), custom_call_target="Cholesky" | custom-call | tf_op jit(solution)/shard_map/jit(cholesky)/cholesky | solution.py:45
  536.5 22.4 %while.1 = (s32[]{:T(128)}, f32[1024,1024]{1,0:T(8,128)}, s32[8,2]{0,1:T(2,128)S(1)}, f32[8,128,128]{2,1,0:T(8,128)S(1)}, s32[]{:T(128)}) while((s32[]{:T(128)}, f32[1024,1024]{1,0:T(8,128)}, s32[8,2]{0,1:T(2,128)S(1)}, f32[8,128,128]{2,1,0:T(8,128)S(1)}, s32[]{:T(128)}) %tuple.76), condition=%wide.while_cond, body=%wide.while_body.sunk | while | flops 2 | bytes 131181 | solution.py:47
  558.9 78.8 %custom-call.71 = f32[8,128,128]{1,2,0:T(8,128)S(1)} custom-call(f32[8,128,128]{2,1,0:T(8,128)S(1)} %get-tuple-element.12), custom_call_target="InvertDiagBlocksLowerTriangular" | custom-call | tf_op jit(solution)/shard_map/triangular_solve | solution.py:47
  660.1 25.5 %convolution_add_fusion = f32[64,8192]{1,0:T(8,128)} fusion(f32[64,8192]{1,0:T(8,128)S(1)} %copy-done, f32[1024,64]{0,1:T(8,128)S(1)} %constant_dynamic-update-slice_fusion.36, f32[1024,8192]{1,0:T(8,128)} %all-gather.8.cloned.1.call-done), kind=kOutput, calls=%fused_computation.2 | convolution fusion | flops 6442975232 | bytes 38010880 | tf_op jit(solution)/shard_map/kj,kc->jc/dot_general | solution.py:98
  (165 shorter events, 126.7 us)
Async XLA Ops:
  6.5 174.3 %all-gather.4.cloned.1.call-start = ((), (), s32[]{:S(2)}) async-start(), calls=%async_computation | async-start | bytes 8912896 | tf_op jit(solution)/shard_map/all_gather | solution.py:91
  24.5 72.8 %copy-start.2 = (f32[2048]{0:T(1024)S(1)}, f32[2048]{0:T(1024)}, u32[]{:S(2)}) copy-start(f32[2048]{0:T(1024)} %param.20) | copy-start | bytes 24580
  24.5 72.8 %copy-start.3 = (f32[2048]{0:T(1024)S(1)}, f32[2048]{0:T(1024)}, u32[]{:S(2)}) copy-start(f32[2048]{0:T(1024)} %param.19) | copy-start | bytes 24580
  99.3 159.0 %all-reduce.4.cloned.1.call-start = ((), (), s32[]{:S(2)}) async-start(), calls=%async_computation.1 | async-start | bytes 1048576 | tf_op jit(solution)/shard_map/psum | solution.py:92
  180.8 79.4 %copy-start = (f32[64,8192]{1,0:T(8,128)S(1)}, f32[64,8192]{1,0:T(8,128)}, u32[]{:S(2)}) copy-start(f32[64,8192]{1,0:T(8,128)} %param.11) | copy-start | bytes 6291460
  192.8 116.3 %all-gather.6.cloned.1.call-start = ((), (), s32[]{:S(2)}) async-start(), calls=%async_computation.2 | async-start | bytes 4456448 | tf_op jit(solution)/shard_map/all_gather | solution.py:93
  260.1 399.9 %all-gather.8.cloned.1.call-start = ((), (), s32[]{:S(2)}) async-start(), calls=%async_computation.3 | async-start | bytes 35651584 | tf_op jit(solution)/shard_map/all_gather | solution.py:101
  325.6 2.0 copy-start.1
Sparse Core Ops, SparseCore 0:
  99.4 81.3 all-gather.3
  192.9 58.3 all-reduce.3
  260.2 48.8 all-gather.5
  311.3 197.7 all-gather.7
where the time goes:
time: 701 us; the launch traced here: 692 us
  other arithmetic  282 us (40%)
  waiting for transfers between devices  129 us (18%)
  blocking collectives  127 us (18%)
  matrix products  92.4 us (13%)
  local copies, waits for them, and re-layouts  41.4 us (6%)
  between operations  20.1 us (3%)
    another operation x30, other arithmetic, spd_solve(): factor = jnp.linalg.cholesky(matrix)  173 us
    another operation x3, other arithmetic, spd_solve(): lax.linalg.triangular_solve(factor, halfway, left_side=True, lower=True,...  83.7 us
    all_gather x1, waiting for transfers between devices, body(): lax.all_gather(pred_anomaly, 'mem', axis=0, tiled=True)  81.4 us
    psum x1, blocking collectives, body(): misfit_sum = lax.psum(misfit_local, ('mem', 'cell'))  64.7 us
    psum x1, blocking collectives, body(): lax.psum((jnp.sum(turnover_effect, axis=0), jnp.sum(predicted, axis=0)),...  62.6 us
    all_gather x1, waiting for transfers between devices, body(): gram = lax.all_gather(summed[:, :local_members], 'mem', axis=1, tiled=True)  47.4 us
    dot_general x1, matrix products, body(): jnp.einsum('kj,kc->jc', local_solve, lax.all_gather(anomaly, 'mem', axis=...  25.5 us
    another operation x14, matrix products, spd_solve(): factor = jnp.linalg.cholesky(matrix)  23.2 us
  transfers between devices with their start and end apart: 4, of which 2 were waited for; matrix products, arithmetic and copies ran while one was open for 50% of the time, Pallas kernels for 0%

commit v1 on v0

--- a/solution.py
+++ b/solution.py
@@ -8,6 +8,22 @@
 BLOCK = 128
 TAPS = 4
 highest = lax.Precision.HIGHEST
+
+
+def gather_around(x, axis, dim):
+    ways, here, hop = (lax.axis_size(axis), lax.axis_index(axis), x.shape[dim])
+    shape = [n * ways if d == dim else n for d, n in enumerate(x.shape)]
+    full = lax.dynamic_update_slice_in_dim(jnp.zeros(shape, x.dtype), x, here * hop, axis=dim)
+    going_up = going_down = x
+    for far in range(1, ways // 2 + 1):
+        going_up = lax.ppermute(going_up, axis, [(d, (d + 1) % ways) for d in range(ways)])
+        full = lax.dynamic_update_slice_in_dim(full, going_up, (here - far) % ways * hop, axis=dim)
+        if 2 * far < ways:
+            going_down = lax.ppermute(going_down, axis, [(d, (d - 1) % ways) for d in range(ways)])
+            full = lax.dynamic_update_slice_in_dim(
+                full, going_down, (here + far) % ways * hop, axis=dim
+            )
+    return full
 
 
 def forward(turnover_effect, base_rate, fast_rate, slow_rate, init_pools, litterfall):
@@ -88,7 +104,7 @@
     stacked = jnp.concatenate(
         [pred_anomaly / obs_var[None, :], departure / obs_var[None, :]], axis=0
     )
-    partial_cols = contract_last(lax.all_gather(pred_anomaly, "mem", axis=0, tiled=True), stacked)
+    partial_cols = contract_last(gather_around(pred_anomaly, "mem", 0), stacked)
     summed = lax.psum(partial_cols, "cell")
     gram = lax.all_gather(summed[:, :local_members], "mem", axis=1, tiled=True)
     step_size = member_count * all_obs / misfit_sum

time: 701 us -> 742 us (1.058)
  starting transfers between devices: 0.13 us -> 35.7 us
  waiting for transfers between devices: 129 us -> 98.7 us
  local copies, waits for them, and re-layouts: 41.4 us -> 62.3 us
  blocking collectives: 127 us -> 142 us
    all_gather x1 -> x0, waiting for transfers between devices: 81.4 us -> none  [body(): lax.all_gather(pred_anomaly, 'mem', axis=0, tiled=True)]
    ppermute x0 -> x15, waiting for transfers between devices: none -> 51.2 us  [the longest x8 28.1 us: gather_around(): lax.ppermute(going_up, axis, [(d, (d + 1) % ways) for d in range(ways)])]
    ppermute x0 -> x15, starting transfers between devices: none -> 35.6 us  [the longest x7 35.4 us: gather_around(): lax.ppermute(going_down, axis, [(d, (d - 1) % ways) for d in range(ways)])]
    dynamic_update_slice x0 -> x16, local copies, waits for them, and re-layouts: none -> 17.7 us  [the longest x8 8.84 us: gather_around(): lax.dynamic_update_slice_in_dim(full, going_up, (here - far) % ways * hop...]
    psum x1, blocking collectives: 64.7 us -> 79.7 us  [body(): misfit_sum = lax.psum(misfit_local, ('mem', 'cell'))]
  transfers between devices with their start and end apart: 4 -> 18, of which waited for: 2 -> 9; matrix products, arithmetic and copies ran while one was open for 50% -> 50% of each run, Pallas kernels for 0% -> 0%
where the time goes in v1:
time: 742 us; the launch traced here: 732 us
  other arithmetic  280 us (38%)
  blocking collectives  142 us (19%)
  waiting for transfers between devices  98.7 us (13%)
  matrix products  92.4 us (12%)
  local copies, waits for them, and re-layouts  62.3 us (8%)
  starting transfers between devices  35.7 us (5%)
  between operations  20.1 us (3%)
    another operation x30, other arithmetic, spd_solve(): factor = jnp.linalg.cholesky(matrix)  173 us
    another operation x3, other arithmetic, spd_solve(): lax.linalg.triangular_solve(factor, halfway, left_side=True, lower=True,...  83.7 us
    psum x1, blocking collectives, body(): misfit_sum = lax.psum(misfit_local, ('mem', 'cell'))  79.7 us
    psum x1, blocking collectives, body(): lax.psum((jnp.sum(turnover_effect, axis=0), jnp.sum(predicted, axis=0)),...  62.6 us
    all_gather x1, waiting for transfers between devices, body(): gram = lax.all_gather(summed[:, :local_members], 'mem', axis=1, tiled=True)  47.4 us
    ppermute x7, starting transfers between devices, gather_around(): lax.ppermute(going_down, axis, [(d, (d - 1) % ways) for d in range(ways)])  35.4 us
    ppermute x8, waiting for transfers between devices, gather_around(): lax.ppermute(going_up, axis, [(d, (d + 1) % ways) for d in range(ways)])  28.1 us
    dot_general x1, matrix products, body(): jnp.einsum('kj,kc->jc', local_solve, lax.all_gather(anomaly, 'mem', axis=...  25.5 us
  transfers between devices with their start and end apart: 18, of which 9 were waited for; matrix products, arithmetic and copies ran while one was open for 50% of the time, Pallas kernels for 0%

profile of v1, /device:TPU:1, one launch (start us, length us, event | category | flops | bytes accessed | tf_op | source)
XLA Modules:
  0.0 732.1 jit_solution(17211580333655776428)
XLA Ops:
  23.9 9.8 %fusion.32 = (f32[]{:T(128)}, f32[64,32]{1,0:T(8,128)S(1)}, f32[64,32,64]{2,1,0:T(8,128)S(1)}) fusion(f32[64,32]{1,0:T(8,128)S(1)} %div.48, f32[64,32]{1,0:T(8,128)S(1)} %sub.108, f32[8,64,8,128]{3,2,1,0:T(8,128)S(1)} %get-tuple-element.42, f32[64,32]{1,0:T(8,128)S(1)} %mul.316, s32[64,32]{1,0:T(8,128)S(1)} %eq.96, f32[64,32]{1,0:T(8,128)S(1)} %mul.313, ...), kind=kOutput, calls=%fused_computation.81 | convolution fusion | flops 204863488 | bytes 2711556 | tf_op jit(solution)/shard_map/jbc,boc->jbo/dot_general | solution.py:56
  33.8 62.6 %all-reduce.1 = (f32[2048]{0:T(1024)S(1)}, f32[8192]{0:T(1024)S(1)}) all-reduce(f32[2048]{0:T(1024)S(1)} %reduce_sum.31, f32[8192]{0:T(1024)S(1)} %get-tuple-element.41), channel_id=1, replica_groups=mesh['mem'=16,'cell'=8] {'mem'}, use_global_device_ids=true, to_apply=%region_3.0 | all-reduce | flops 10240 | bytes 81920 | tf_op jit(solution)/shard_map/psum | solution.py:94
  113.2 8.4 %collective-permute-done.2 = f32[64,2048]{1,0:T(8,128)S(1)} collective-permute-done((f32[64,2048]{1,0:T(8,128)S(1)}, f32[64,2048]{1,0:T(8,128)S(1)}, u32[]{:S(2)}, u32[]{:S(2)}) %collective-permute-start.2) | collective-permute-done | bytes 524320 | tf_op jit(solution)/shard_map/ppermute | solution.py:19
  205.7 12.0 %fusion.19 = f32[1024,128]{0,1:T(8,128)} fusion(f32[1024,2048]{1,0:T(8,128)} %constant_dynamic-update-slice_fusion.44, f32[64,2048]{1,0:T(8,128)S(1)} %get-tuple-element.43, f32[64,2048]{1,0:T(8,128)S(1)} %get-tuple-element.33), kind=kOutput, calls=%fused_computation.62 | convolution fusion | flops 3221487616 | bytes 9961472 | tf_op jit(solution)/shard_map/dot_general | solution.py:69
  217.8 79.7 %psum.28 = f32[]{:T(128)} all-reduce(f32[]{:T(128)} %get-tuple-element.13), channel_id=1, replica_groups=mesh['mem'=16,'cell'=8] {'mem','cell'}, use_global_device_ids=true, to_apply=%region_1.0 | all-reduce | flops 1 | bytes 8 | tf_op jit(solution)/shard_map/psum | solution.py:103
  301.7 47.4 %all-gather.3.cloned.1.call-done = f32[1024,1024]{0,1:T(8,128)} async-done(((f32[1024,64]{0,1:T(8,128)}), f32[1024,1024]{0,1:T(8,128)}) %all-gather.3.cloned.1.call-update) | async-done | bytes 4194320 | tf_op jit(solution)/shard_map/all_gather | solution.py:109
  367.2 11.7 %cholesky.223 = f32[128,128]{1,0:T(8,128)S(1)} custom-call(f32[128,128]{1,0:T(8,128)S(1)} %cholesky.580), custom_call_target="Cholesky" | custom-call | tf_op jit(solution)/shard_map/jit(cholesky)/cholesky | solution.py:61
  381.4 9.8 %custom-call.64 = f32[1,128,128]{1,2,0:T(8,128)S(1)} custom-call(f32[1,128,128]{2,1,0:T(8,128)S(1)} %get-tuple-element.75), custom_call_target="InvertDiagBlocksLowerTriangular" | custom-call | tf_op jit(solution)/shard_map/jit(cholesky)/cholesky | solution.py:61
  395.2 12.1 %cholesky.244 = f32[128,128]{1,0:T(8,128)S(1)} custom-call(f32[128,128]{1,0:T(8,128)S(1)} %cholesky.584), custom_call_target="Cholesky" | custom-call | tf_op jit(solution)/shard_map/jit(cholesky)/cholesky | solution.py:61
  407.9 9.8 %custom-call.65 = f32[1,128,128]{1,2,0:T(8,128)S(1)} custom-call(f32[1,128,128]{2,1,0:T(8,128)S(1)} %get-tuple-element.72), custom_call_target="InvertDiagBlocksLowerTriangular" | custom-call | tf_op jit(solution)/shard_map/jit(cholesky)/cholesky | solution.py:61
  421.1 11.7 %cholesky.468 = f32[128,128]{1,0:T(8,128)S(1)} custom-call(f32[128,128]{1,0:T(8,128)S(1)} %cholesky.589), custom_call_target="Cholesky" | custom-call | tf_op jit(solution)/shard_map/jit(cholesky)/cholesky | solution.py:61
  433.5 9.8 %custom-call.66 = f32[1,128,128]{1,2,0:T(8,128)S(1)} custom-call(f32[1,128,128]{2,1,0:T(8,128)S(1)} %get-tuple-element.69), custom_call_target="InvertDiagBlocksLowerTriangular" | custom-call | tf_op jit(solution)/shard_map/jit(cholesky)/cholesky | solution.py:61
  446.8 11.9 %cholesky.487 = f32[128,128]{1,0:T(8,128)S(1)} custom-call(f32[128,128]{1,0:T(8,128)S(1)} %cholesky.594), custom_call_target="Cholesky" | custom-call | tf_op jit(solution)/shard_map/jit(cholesky)/cholesky | solution.py:61
  459.3 9.8 %custom-call.67 = f32[1,128,128]{1,2,0:T(8,128)S(1)} custom-call(f32[1,128,128]{2,1,0:T(8,128)S(1)} %get-tuple-element.66), custom_call_target="InvertDiagBlocksLowerTriangular" | custom-call | tf_op jit(solution)/shard_map/jit(cholesky)/cholesky | solution.py:61
  472.6 11.7 %cholesky.506 = f32[128,128]{1,0:T(8,128)S(1)} custom-call(f32[128,128]{1,0:T(8,128)S(1)} %cholesky.599), custom_call_target="Cholesky" | custom-call | tf_op jit(solution)/shard_map/jit(cholesky)/cholesky | solution.py:61
  485.0 10.0 %custom-call.68 = f32[1,128,128]{1,2,0:T(8,128)S(1)} custom-call(f32[1,128,128]{2,1,0:T(8,128)S(1)} %get-tuple-element.63), custom_call_target="InvertDiagBlocksLowerTriangular" | custom-call | tf_op jit(solution)/shard_map/jit(cholesky)/cholesky | solution.py:61
  498.4 11.7 %cholesky.526 = f32[128,128]{1,0:T(8,128)S(1)} custom-call(f32[128,128]{1,0:T(8,128)S(1)} %cholesky.604), custom_call_target="Cholesky" | custom-call | tf_op jit(solution)/shard_map/jit(cholesky)/cholesky | solution.py:61
  510.7 9.8 %custom-call.69 = f32[1,128,128]{1,2,0:T(8,128)S(1)} custom-call(f32[1,128,128]{2,1,0:T(8,128)S(1)} %get-tuple-element.60), custom_call_target="InvertDiagBlocksLowerTriangular" | custom-call | tf_op jit(solution)/shard_map/jit(cholesky)/cholesky | solution.py:61
  523.5 12.1 %cholesky.546 = f32[128,128]{1,0:T(8,128)S(1)} custom-call(f32[128,128]{1,0:T(8,128)S(1)} %cholesky.609), custom_call_target="Cholesky" | custom-call | tf_op jit(solution)/shard_map/jit(cholesky)/cholesky | solution.py:61
  536.3 9.8 %custom-call.70 = f32[1,128,128]{1,2,0:T(8,128)S(1)} custom-call(f32[1,128,128]{2,1,0:T(8,128)S(1)} %get-tuple-element.57), custom_call_target="InvertDiagBlocksLowerTriangular" | custom-call | tf_op jit(solution)/shard_map/jit(cholesky)/cholesky | solution.py:61
  548.8 11.7 %cholesky.564 = f32[128,128]{1,0:T(8,128)S(1)} custom-call(f32[128,128]{1,0:T(8,128)S(1)} %convolution_subtract_fusion.6), custom_call_target="Cholesky" | custom-call | tf_op jit(solution)/shard_map/jit(cholesky)/cholesky | solution.py:61
  576.3 22.4 %while.1 = (s32[]{:T(128)}, f32[1024,1024]{1,0:T(8,128)}, s32[8,2]{0,1:T(2,128)S(1)}, f32[8,128,128]{2,1,0:T(8,128)S(1)}, s32[]{:T(128)}) while((s32[]{:T(128)}, f32[1024,1024]{1,0:T(8,128)}, s32[8,2]{0,1:T(2,128)S(1)}, f32[8,128,128]{2,1,0:T(8,128)S(1)}, s32[]{:T(128)}) %tuple.76), condition=%wide.while_cond, body=%wide.while_body.sunk | while | flops 2 | bytes 131181 | solution.py:63
  598.7 78.8 %custom-call.71 = f32[8,128,128]{1,2,0:T(8,128)S(1)} custom-call(f32[8,128,128]{2,1,0:T(8,128)S(1)} %get-tuple-element.12), custom_call_target="InvertDiagBlocksLowerTriangular" | custom-call | tf_op jit(solution)/shard_map/triangular_solve | solution.py:63
  699.8 25.5 %convolution_add_fusion = f32[64,8192]{1,0:T(8,128)} fusion(f32[64,8192]{1,0:T(8,128)S(1)} %copy-done, f32[1024,64]{0,1:T(8,128)S(1)} %constant_dynamic-update-slice_fusion.36, f32[1024,8192]{1,0:T(8,128)} %all-gather.5.cloned.1.call-done), kind=kOutput, calls=%fused_computation.2 | convolution fusion | flops 6442975232 | bytes 38010880 | tf_op jit(solution)/shard_map/kj,kc->jc/dot_general | solution.py:114
  (215 shorter events, 224.3 us)
Async XLA Ops:
  6.5 291.7 %all-reduce.4.cloned.1.call-start = ((), (), s32[]{:S(2)}) async-start(), calls=%async_computation | async-start | bytes 1048576 | tf_op jit(solution)/shard_map/psum | solution.py:108
  23.9 72.8 %copy-start.4 = (f32[64,2048]{1,0:T(8,128)S(1)}, f32[64,2048]{1,0:T(8,128)}, u32[]{:S(2)}) copy-start(f32[64,2048]{1,0:T(8,128)} %param.21) | copy-start | bytes 1572868
  23.9 72.8 %copy-start.5 = (f32[2048]{0:T(1024)S(1)}, f32[2048]{0:T(1024)}, u32[]{:S(2)}) copy-start(f32[2048]{0:T(1024)} %param.20) | copy-start | bytes 24580
  23.9 72.8 %copy-start.6 = (f32[2048]{0:T(1024)S(1)}, f32[2048]{0:T(1024)}, u32[]{:S(2)}) copy-start(f32[2048]{0:T(1024)} %param.19) | copy-start | bytes 24580
  96.9 11.5 %collective-permute-start = (f32[64,2048]{1,0:T(8,128)S(1)}, f32[64,2048]{1,0:T(8,128)S(1)}, u32[]{:S(2)}, u32[]{:S(2)}) collective-permute-start(f32[64,2048]{1,0:T(8,128)S(1)} %get-tuple-element.34), channel_id=1, source_target_pairs={{0,8},{8,16},{16,24},{24,32},{32,40},{40,48},{48,56},{56,64},{64,7... | collective-permute-start | bytes 1572872 | tf_op jit(solution)/shard_map/ppermute | solution.py:19
  97.0 11.4 %collective-permute-start.1 = (f32[64,2048]{1,0:T(8,128)S(1)}, f32[64,2048]{1,0:T(8,128)S(1)}, u32[]{:S(2)}, u32[]{:S(2)}) collective-permute-start(f32[64,2048]{1,0:T(8,128)S(1)} %get-tuple-element.34), channel_id=1, source_target_pairs={{0,120},{8,0},{16,8},{24,16},{32,24},{40,32},{48,40},{56,48},{64,5... | collective-permute-start | bytes 1572872 | tf_op jit(solution)/shard_map/ppermute | solution.py:22
  108.4 4.8 copy-start.3
  108.4 13.2 %collective-permute-start.2 = (f32[64,2048]{1,0:T(8,128)S(1)}, f32[64,2048]{1,0:T(8,128)S(1)}, u32[]{:S(2)}, u32[]{:S(2)}) collective-permute-start(f32[64,2048]{1,0:T(8,128)S(1)} %collective-permute-done), channel_id=1, source_target_pairs={{0,8},{8,16},{16,24},{24,32},{32,40},{40,48},{48,56},{56,64},{64,7... | collective-permute-start | bytes 1572872 | tf_op jit(solution)/shard_map/ppermute | solution.py:19
  108.4 13.2 %copy-start.2 = (f32[64,2048]{1,0:T(8,128)}, f32[64,2048]{1,0:T(8,128)S(1)}, u32[]{:S(2)}) copy-start(f32[64,2048]{1,0:T(8,128)S(1)} %collective-permute-done.1) | copy-start | bytes 1572868
  108.4 13.2 %collective-permute-start.3 = (f32[64,2048]{1,0:T(8,128)S(1)}, f32[64,2048]{1,0:T(8,128)}, u32[]{:S(2)}, u32[]{:S(2)}) collective-permute-start(f32[64,2048]{1,0:T(8,128)S(1)} %collective-permute-done.1), channel_id=1, source_target_pairs={{0,120},{8,0},{16,8},{24,16},{32,24},{40,32},{48,40},{56,48},{64,5... | collective-permute-start | bytes 1572872 | tf_op jit(solution)/shard_map/ppermute | solution.py:22
  121.6 12.3 %collective-permute-start.4 = (f32[64,2048]{1,0:T(8,128)S(1)}, f32[64,2048]{1,0:T(8,128)S(1)}, u32[]{:S(2)}, u32[]{:S(2)}) collective-permute-start(f32[64,2048]{1,0:T(8,128)S(1)} %collective-permute-done.2), channel_id=1, source_target_pairs={{0,8},{8,16},{16,24},{24,32},{32,40},{40,48},{48,56},{56,64},{64,7... | collective-permute-start | bytes 1572872 | tf_op jit(solution)/shard_map/ppermute | solution.py:19
  121.6 19.3 %collective-permute-start.5 = (f32[64,2048]{1,0:T(8,128)}, f32[64,2048]{1,0:T(8,128)S(1)}, u32[]{:S(2)}, u32[]{:S(2)}) collective-permute-start(f32[64,2048]{1,0:T(8,128)} %collective-permute-done.3), channel_id=1, source_target_pairs={{0,120},{8,0},{16,8},{24,16},{32,24},{40,32},{48,40},{56,48},{64,5... | collective-permute-start | bytes 1572872 | tf_op jit(solution)/shard_map/ppermute | solution.py:22
  133.9 13.7 %collective-permute-start.6 = (f32[64,2048]{1,0:T(8,128)S(1)}, f32[64,2048]{1,0:T(8,128)}, u32[]{:S(2)}, u32[]{:S(2)}) collective-permute-start(f32[64,2048]{1,0:T(8,128)S(1)} %collective-permute-done.4), channel_id=1, source_target_pairs={{0,8},{8,16},{16,24},{24,32},{32,40},{40,48},{48,56},{56,64},{64,7... | collective-permute-start | bytes 1572872 | tf_op jit(solution)/shard_map/ppermute | solution.py:19
  140.9 15.9 %collective-permute-start.7 = (f32[64,2048]{1,0:T(8,128)S(1)}, f32[64,2048]{1,0:T(8,128)S(1)}, u32[]{:S(2)}, u32[]{:S(2)}) collective-permute-start(f32[64,2048]{1,0:T(8,128)S(1)} %collective-permute-done.5), channel_id=1, source_target_pairs={{0,120},{8,0},{16,8},{24,16},{32,24},{40,32},{48,40},{56,48},{64,5... | collective-permute-start | bytes 1572872 | tf_op jit(solution)/shard_map/ppermute | solution.py:22
  147.5 15.3 %collective-permute-start.8 = (f32[64,2048]{1,0:T(8,128)}, f32[64,2048]{1,0:T(8,128)S(1)}, u32[]{:S(2)}, u32[]{:S(2)}) collective-permute-start(f32[64,2048]{1,0:T(8,128)} %collective-permute-done.6), channel_id=1, source_target_pairs={{0,8},{8,16},{16,24},{24,32},{32,40},{40,48},{48,56},{56,64},{64,7... | collective-permute-start | bytes 1572872 | tf_op jit(solution)/shard_map/ppermute | solution.py:19
  156.8 14.6 %collective-permute-start.9 = (f32[64,2048]{1,0:T(8,128)S(1)}, f32[64,2048]{1,0:T(8,128)S(1)}, u32[]{:S(2)}, u32[]{:S(2)}) collective-permute-start(f32[64,2048]{1,0:T(8,128)S(1)} %collective-permute-done.7), channel_id=1, source_target_pairs={{0,120},{8,0},{16,8},{24,16},{32,24},{40,32},{48,40},{56,48},{64,5... | collective-permute-start | bytes 1572872 | tf_op jit(solution)/shard_map/ppermute | solution.py:22
  162.9 14.9 %collective-permute-start.10 = (f32[64,2048]{1,0:T(8,128)S(1)}, f32[64,2048]{1,0:T(8,128)S(1)}, u32[]{:S(2)}, u32[]{:S(2)}) collective-permute-start(f32[64,2048]{1,0:T(8,128)S(1)} %collective-permute-done.8), channel_id=1, source_target_pairs={{0,8},{8,16},{16,24},{24,32},{32,40},{40,48},{48,56},{56,64},{64,7... | collective-permute-start | bytes 1572872 | tf_op jit(solution)/shard_map/ppermute | solution.py:19
  171.4 14.0 %collective-permute-start.11 = (f32[64,2048]{1,0:T(8,128)S(1)}, f32[64,2048]{1,0:T(8,128)S(1)}, u32[]{:S(2)}, u32[]{:S(2)}) collective-permute-start(f32[64,2048]{1,0:T(8,128)S(1)} %collective-permute-done.9), channel_id=1, source_target_pairs={{0,120},{8,0},{16,8},{24,16},{32,24},{40,32},{48,40},{56,48},{64,5... | collective-permute-start | bytes 1572872 | tf_op jit(solution)/shard_map/ppermute | solution.py:22
  177.8 14.0 %collective-permute-start.12 = (f32[64,2048]{1,0:T(8,128)S(1)}, f32[64,2048]{1,0:T(8,128)S(1)}, u32[]{:S(2)}, u32[]{:S(2)}) collective-permute-start(f32[64,2048]{1,0:T(8,128)S(1)} %collective-permute-done.10), channel_id=1, source_target_pairs={{0,8},{8,16},{16,24},{24,32},{32,40},{40,48},{48,56},{56,64},{64,7... | collective-permute-start | bytes 1572872 | tf_op jit(solution)/shard_map/ppermute | solution.py:19
  185.4 13.1 %collective-permute-start.13 = (f32[64,2048]{1,0:T(8,128)S(1)}, f32[64,2048]{1,0:T(8,128)S(1)}, u32[]{:S(2)}, u32[]{:S(2)}) collective-permute-start(f32[64,2048]{1,0:T(8,128)S(1)} %collective-permute-done.11), channel_id=1, source_target_pairs={{0,120},{8,0},{16,8},{24,16},{32,24},{40,32},{48,40},{56,48},{64,5... | collective-permute-start | bytes 1572872 | tf_op jit(solution)/shard_map/ppermute | solution.py:22
  191.8 13.1 %collective-permute-start.14 = (f32[64,2048]{1,0:T(8,128)S(1)}, f32[64,2048]{1,0:T(8,128)S(1)}, u32[]{:S(2)}, u32[]{:S(2)}) collective-permute-start(f32[64,2048]{1,0:T(8,128)S(1)} %collective-permute-done.12), channel_id=1, source_target_pairs={{0,8},{8,16},{16,24},{24,32},{32,40},{40,48},{48,56},{56,64},{64,7... | collective-permute-start | bytes 1572872 | tf_op jit(solution)/shard_map/ppermute | solution.py:19
  205.7 94.4 %copy-start = (f32[64,8192]{1,0:T(8,128)S(1)}, f32[64,8192]{1,0:T(8,128)}, u32[]{:S(2)}) copy-start(f32[64,8192]{1,0:T(8,128)} %param.11) | copy-start | bytes 6291460
  217.7 131.3 %all-gather.3.cloned.1.call-start = ((), (), s32[]{:S(2)}) async-start(), calls=%async_computation.1 | async-start | bytes 4456448 | tf_op jit(solution)/shard_map/all_gather | solution.py:109
  300.0 399.8 %all-gather.5.cloned.1.call-start = ((), (), s32[]{:S(2)}) async-start(), calls=%async_computation.2 | async-start | bytes 35651584 | tf_op jit(solution)/shard_map/all_gather | solution.py:117
  (1 other events, 2.0 us)
Sparse Core Ops, SparseCore 0:
  217.9 71.6 all-reduce.3
  300.2 48.8 all-gather.2
  351.4 197.1 all-gather.4
